TPU v7x, 128 devices: a whole 4x4x4 slice. The times are simulated.
128 devices in a mesh: grp: 4 (over x), seq: 32 (over y, z, core).
Axes of the slice: x: 4, y: 4, z: 4, core: 2. Of those that a mesh axis runs over, the one named last changes fastest.
Arguments:
- lin_q: bfloat16 [8192, 8192], P('seq', 'grp'), may hold values from -6 to 6
- lin_k: bfloat16 [8192, 8192], P('seq', 'grp'), may hold values from -6 to 6
- lin_v: bfloat16 [8192, 8192], P('seq', 'grp'), may hold values from -60 to 60
- lin_gain: float32 [8192], P('grp'), may hold values from 0.1 to 1.9
- soft_q: bfloat16 [8192, 8192], P('seq', 'grp'), may hold values from -6 to 6
- soft_k: bfloat16 [8192, 8192], P('seq', 'grp'), may hold values from -12.5 to 12.5
- soft_v: bfloat16 [8192, 8192], P('seq', 'grp'), may hold values from -6 to 6
Outputs:
- lin_out: bfloat16 [8192, 8192], P('seq', 'grp')
- soft_out: bfloat16 [8192, 8192], P('seq', 'grp')
All inputs are finite; a program needn't handle non-finite values.
Results may differ from a plain program's by a relative error of at most 0.0031.
Values may be sent and summed in bfloat16 or wider, within the bound.
A program may use at most 192 MiB of HBM per device.

v0:
```python
import jax
import jax.numpy as jnp
from jax import lax
from jax.sharding import PartitionSpec as P

HEADS = 64
HEAD_DIM = 128


highest = lax.Precision.HIGHEST
epsilon = 1e-06


def from_behind(value, axis, by):
    peers = lax.axis_size(axis)
    pairs = [(i, i + by) for i in range(peers) if 0 <= i + by < peers]
    return lax.ppermute(value, axis, pairs)


def shards(lin_q, lin_k, lin_v, lin_gain, soft_q, soft_k, soft_v):
    rows_dev, width_dev = lin_q.shape
    head_size = HEAD_DIM
    local_heads = width_dev // head_size
    queries_low = lin_q.reshape(rows_dev, local_heads, head_size)
    keys_low = lin_k.reshape(rows_dev, local_heads, head_size)
    values_low = lin_v.reshape(rows_dev, local_heads, head_size)
    queries = queries_low.astype(jnp.float32)
    values_lin = values_low.astype(jnp.float32)
    own_state = jnp.einsum("thd,the->hde", keys_low, values_low, preferred_element_type=jnp.float32)
    zero_state = jnp.zeros_like(own_state)

    def relay_step(counter, running):
        return from_behind(running + own_state, "seq", 1)

    prefix = lax.fori_loop(0, lax.axis_size("seq") - 1, relay_step, zero_state)
    row_ids = lax.broadcasted_iota(jnp.int32, (rows_dev, rows_dev), 0)
    col_ids = lax.broadcasted_iota(jnp.int32, (rows_dev, rows_dev), 1)
    causal = (col_ids <= row_ids).astype(jnp.float32)
    scores_lin = (
        jnp.einsum("thd,shd->hts", queries_low, keys_low, preferred_element_type=jnp.float32)
        * causal[None]
    )
    within = jnp.einsum("hts,she->the", scores_lin, values_lin, precision=highest)
    carried = jnp.einsum("thd,hde->the", queries, prefix, precision=highest)
    mixed_out = (within + carried).reshape(rows_dev, width_dev)
    squares = jnp.sum(mixed_out * mixed_out, axis=1)
    summed = lax.psum(squares, "grp")
    inverse = lax.rsqrt(summed / (HEADS * head_size) + epsilon)
    lin_out = (mixed_out * inverse[:, None] * lin_gain).astype(jnp.bfloat16)
    seq_devices = lax.axis_size("seq")
    seq_index = lax.axis_index("seq")
    units = 2 * local_heads // seq_devices
    half_rows = rows_dev // 2
    query_units = (
        soft_q.reshape(2, half_rows, local_heads, head_size)
        .transpose(2, 0, 1, 3)
        .reshape(2 * local_heads, half_rows, head_size)
    )

    def head_pieces(source):
        shaped = source.reshape(rows_dev, local_heads, head_size)
        shaped = jnp.repeat(shaped, 2, axis=1)
        return shaped.transpose(1, 0, 2)

    query_in, keys_in, values_in = (
        lax.all_to_all(query_units, "seq", split_axis=0, concat_axis=1, tiled=True),
        lax.all_to_all(head_pieces(soft_k), "seq", split_axis=0, concat_axis=1, tiled=True),
        lax.all_to_all(head_pieces(soft_v), "seq", split_axis=0, concat_axis=1, tiled=True),
    )
    seq_len = seq_devices * rows_dev
    query_rows = seq_len // 2
    block_rows = query_rows // 8
    scale = head_size ** (-0.5)
    half_index = (seq_index * units + 0) % 2
    head_slot = 0 // 2
    pieces = []
    for block_index in range(8):
        key_count = (block_index + 1) * seq_len // 8
        block_q = query_in[0, block_index * block_rows : (block_index + 1) * block_rows]
        block_k = keys_in[head_slot, :key_count]
        block_v = values_in[head_slot, :key_count]
        scores = (
            jnp.einsum("qd,kd->qk", block_q, block_k, preferred_element_type=jnp.float32) * scale
        )
        local_rows = block_index * block_rows + lax.broadcasted_iota(jnp.int32, (block_rows, 1), 0)
        positions_q = (
            local_rows // half_rows * rows_dev + half_index * half_rows + local_rows % half_rows
        )
        positions_k = lax.broadcasted_iota(jnp.int32, (1, key_count), 1)
        scores = jnp.where(positions_k <= positions_q, scores, -1e30)
        largest = jnp.max(scores, axis=1, keepdims=True)
        exponent = jnp.exp(scores - largest)
        denominator = jnp.sum(exponent, axis=1, keepdims=True)
        weights = exponent.astype(jnp.bfloat16)
        numerator = jnp.dot(weights, block_v, preferred_element_type=jnp.float32)
        pieces.append((numerator / denominator).astype(jnp.bfloat16))
    outputs = [jnp.concatenate(pieces, axis=0)]
    unit_out = jnp.stack(outputs, axis=0)
    returned = lax.all_to_all(unit_out, "seq", split_axis=1, concat_axis=0, tiled=True)
    soft_out = (
        returned.reshape(local_heads, 2, half_rows, head_size)
        .transpose(1, 2, 0, 3)
        .reshape(rows_dev, width_dev)
    )
    return (lin_out, soft_out)


def solution(mesh):
    return jax.shard_map(
        shards,
        mesh=mesh,
        in_specs=(
            P("seq", "grp"),
            P("seq", "grp"),
            P("seq", "grp"),
            P("grp"),
            P("seq", "grp"),
            P("seq", "grp"),
            P("seq", "grp"),
        ),
        out_specs=(P("seq", "grp"), P("seq", "grp")),
        check_vma=False,
    )
```

profile of v0, /device:TPU:0, one launch (start us, length us, event | category | flops | bytes accessed | tf_op | source)
XLA Modules:
  0.0 863.1 jit_solution(12435779975694789825)
XLA Ops:
  12.5 16.5 %all-to-all-done = bf16[32,128,128]{2,1,0:T(8,128)(2,1)} async-done(((bf16[32,128,128]{2,1,0:T(8,128)(2,1)}), bf16[32,128,128]{2,1,0:T(8,128)(2,1)}, u32[]{:S(2)}, u32[]{:S(2)}) %all-to-all-start) | async-done | bytes 1048608 | tf_op jit(solution)/shard_map/all_to_all | solution.py:66
  40.7 550.3 %while.10 = (s32[]{:T(128)}, f32[16,128,128]{2,1,0:T(8,128)S(1)}, f32[16,128,128]{2,1,0:T(8,128)S(1)}, s32[]{:T(128)}) while((s32[]{:T(128)}, f32[16,128,128]{2,1,0:T(8,128)S(1)}, f32[16,128,128]{2,1,0:T(8,128)S(1)}, s32[]{:T(128)}) %tuple.35), condition=%wide.region_1.0_spmd, body=%wide.region_0.0_spmd.sunk | while | flops 262146 | bytes 7340125 | solution.py:35
  47.5 25.7 %collective-permute-start = (f32[16,128,128]{2,1,0:T(8,128)}, f32[16,128,128]{2,1,0:T(8,128)S(1)}, u32[]{:S(2)}, u32[]{:S(2)}) collective-permute-start(f32[16,128,128]{2,1,0:T(8,128)} %add.628), channel_id=1, source_target_pairs={{0,1},{1,2},{2,3},{3,4},{4,5},{5,6},{6,7},{7,8},{8,9},{9,10},{10,1... | collective-permute-start | bytes 3145736 | tf_op jit(solution)/shard_map/while/body/eval_jaxpr/ppermute | solution.py:17
  76.7 13.9 %collective-permute-start = (f32[16,128,128]{2,1,0:T(8,128)}, f32[16,128,128]{2,1,0:T(8,128)S(1)}, u32[]{:S(2)}, u32[]{:S(2)}) collective-permute-start(f32[16,128,128]{2,1,0:T(8,128)} %add.628), channel_id=1, source_target_pairs={{0,1},{1,2},{2,3},{3,4},{4,5},{5,6},{6,7},{7,8},{8,9},{9,10},{10,1... | collective-permute-start | bytes 3145736 | tf_op jit(solution)/shard_map/while/body/eval_jaxpr/ppermute | solution.py:17
  94.1 13.9 %collective-permute-start = (f32[16,128,128]{2,1,0:T(8,128)}, f32[16,128,128]{2,1,0:T(8,128)S(1)}, u32[]{:S(2)}, u32[]{:S(2)}) collective-permute-start(f32[16,128,128]{2,1,0:T(8,128)} %add.628), channel_id=1, source_target_pairs={{0,1},{1,2},{2,3},{3,4},{4,5},{5,6},{6,7},{7,8},{8,9},{9,10},{10,1... | collective-permute-start | bytes 3145736 | tf_op jit(solution)/shard_map/while/body/eval_jaxpr/ppermute | solution.py:17
  111.6 13.9 %collective-permute-start = (f32[16,128,128]{2,1,0:T(8,128)}, f32[16,128,128]{2,1,0:T(8,128)S(1)}, u32[]{:S(2)}, u32[]{:S(2)}) collective-permute-start(f32[16,128,128]{2,1,0:T(8,128)} %add.628), channel_id=1, source_target_pairs={{0,1},{1,2},{2,3},{3,4},{4,5},{5,6},{6,7},{7,8},{8,9},{9,10},{10,1... | collective-permute-start | bytes 3145736 | tf_op jit(solution)/shard_map/while/body/eval_jaxpr/ppermute | solution.py:17
  129.0 13.9 %collective-permute-start = (f32[16,128,128]{2,1,0:T(8,128)}, f32[16,128,128]{2,1,0:T(8,128)S(1)}, u32[]{:S(2)}, u32[]{:S(2)}) collective-permute-start(f32[16,128,128]{2,1,0:T(8,128)} %add.628), channel_id=1, source_target_pairs={{0,1},{1,2},{2,3},{3,4},{4,5},{5,6},{6,7},{7,8},{8,9},{9,10},{10,1... | collective-permute-start | bytes 3145736 | tf_op jit(solution)/shard_map/while/body/eval_jaxpr/ppermute | solution.py:17
  146.4 13.9 %collective-permute-start = (f32[16,128,128]{2,1,0:T(8,128)}, f32[16,128,128]{2,1,0:T(8,128)S(1)}, u32[]{:S(2)}, u32[]{:S(2)}) collective-permute-start(f32[16,128,128]{2,1,0:T(8,128)} %add.628), channel_id=1, source_target_pairs={{0,1},{1,2},{2,3},{3,4},{4,5},{5,6},{6,7},{7,8},{8,9},{9,10},{10,1... | collective-permute-start | bytes 3145736 | tf_op jit(solution)/shard_map/while/body/eval_jaxpr/ppermute | solution.py:17
  163.8 13.9 %collective-permute-start = (f32[16,128,128]{2,1,0:T(8,128)}, f32[16,128,128]{2,1,0:T(8,128)S(1)}, u32[]{:S(2)}, u32[]{:S(2)}) collective-permute-start(f32[16,128,128]{2,1,0:T(8,128)} %add.628), channel_id=1, source_target_pairs={{0,1},{1,2},{2,3},{3,4},{4,5},{5,6},{6,7},{7,8},{8,9},{9,10},{10,1... | collective-permute-start | bytes 3145736 | tf_op jit(solution)/shard_map/while/body/eval_jaxpr/ppermute | solution.py:17
  181.2 13.9 %collective-permute-start = (f32[16,128,128]{2,1,0:T(8,128)}, f32[16,128,128]{2,1,0:T(8,128)S(1)}, u32[]{:S(2)}, u32[]{:S(2)}) collective-permute-start(f32[16,128,128]{2,1,0:T(8,128)} %add.628), channel_id=1, source_target_pairs={{0,1},{1,2},{2,3},{3,4},{4,5},{5,6},{6,7},{7,8},{8,9},{9,10},{10,1... | collective-permute-start | bytes 3145736 | tf_op jit(solution)/shard_map/while/body/eval_jaxpr/ppermute | solution.py:17
  198.6 13.9 %collective-permute-start = (f32[16,128,128]{2,1,0:T(8,128)}, f32[16,128,128]{2,1,0:T(8,128)S(1)}, u32[]{:S(2)}, u32[]{:S(2)}) collective-permute-start(f32[16,128,128]{2,1,0:T(8,128)} %add.628), channel_id=1, source_target_pairs={{0,1},{1,2},{2,3},{3,4},{4,5},{5,6},{6,7},{7,8},{8,9},{9,10},{10,1... | collective-permute-start | bytes 3145736 | tf_op jit(solution)/shard_map/while/body/eval_jaxpr/ppermute | solution.py:17
  216.0 13.9 %collective-permute-start = (f32[16,128,128]{2,1,0:T(8,128)}, f32[16,128,128]{2,1,0:T(8,128)S(1)}, u32[]{:S(2)}, u32[]{:S(2)}) collective-permute-start(f32[16,128,128]{2,1,0:T(8,128)} %add.628), channel_id=1, source_target_pairs={{0,1},{1,2},{2,3},{3,4},{4,5},{5,6},{6,7},{7,8},{8,9},{9,10},{10,1... | collective-permute-start | bytes 3145736 | tf_op jit(solution)/shard_map/while/body/eval_jaxpr/ppermute | solution.py:17
  233.4 13.9 %collective-permute-start = (f32[16,128,128]{2,1,0:T(8,128)}, f32[16,128,128]{2,1,0:T(8,128)S(1)}, u32[]{:S(2)}, u32[]{:S(2)}) collective-permute-start(f32[16,128,128]{2,1,0:T(8,128)} %add.628), channel_id=1, source_target_pairs={{0,1},{1,2},{2,3},{3,4},{4,5},{5,6},{6,7},{7,8},{8,9},{9,10},{10,1... | collective-permute-start | bytes 3145736 | tf_op jit(solution)/shard_map/while/body/eval_jaxpr/ppermute | solution.py:17
  355.3 13.9 %collective-permute-start = (f32[16,128,128]{2,1,0:T(8,128)}, f32[16,128,128]{2,1,0:T(8,128)S(1)}, u32[]{:S(2)}, u32[]{:S(2)}) collective-permute-start(f32[16,128,128]{2,1,0:T(8,128)} %add.628), channel_id=1, source_target_pairs={{0,1},{1,2},{2,3},{3,4},{4,5},{5,6},{6,7},{7,8},{8,9},{9,10},{10,1... | collective-permute-start | bytes 3145736 | tf_op jit(solution)/shard_map/while/body/eval_jaxpr/ppermute | solution.py:17
  372.7 13.9 %collective-permute-start = (f32[16,128,128]{2,1,0:T(8,128)}, f32[16,128,128]{2,1,0:T(8,128)S(1)}, u32[]{:S(2)}, u32[]{:S(2)}) collective-permute-start(f32[16,128,128]{2,1,0:T(8,128)} %add.628), channel_id=1, source_target_pairs={{0,1},{1,2},{2,3},{3,4},{4,5},{5,6},{6,7},{7,8},{8,9},{9,10},{10,1... | collective-permute-start | bytes 3145736 | tf_op jit(solution)/shard_map/while/body/eval_jaxpr/ppermute | solution.py:17
  390.1 13.9 %collective-permute-start = (f32[16,128,128]{2,1,0:T(8,128)}, f32[16,128,128]{2,1,0:T(8,128)S(1)}, u32[]{:S(2)}, u32[]{:S(2)}) collective-permute-start(f32[16,128,128]{2,1,0:T(8,128)} %add.628), channel_id=1, source_target_pairs={{0,1},{1,2},{2,3},{3,4},{4,5},{5,6},{6,7},{7,8},{8,9},{9,10},{10,1... | collective-permute-start | bytes 3145736 | tf_op jit(solution)/shard_map/while/body/eval_jaxpr/ppermute | solution.py:17
  494.6 15.9 %collective-permute-start = (f32[16,128,128]{2,1,0:T(8,128)}, f32[16,128,128]{2,1,0:T(8,128)S(1)}, u32[]{:S(2)}, u32[]{:S(2)}) collective-permute-start(f32[16,128,128]{2,1,0:T(8,128)} %add.628), channel_id=1, source_target_pairs={{0,1},{1,2},{2,3},{3,4},{4,5},{5,6},{6,7},{7,8},{8,9},{9,10},{10,1... | collective-permute-start | bytes 3145736 | tf_op jit(solution)/shard_map/while/body/eval_jaxpr/ppermute | solution.py:17
  514.1 16.0 %collective-permute-start = (f32[16,128,128]{2,1,0:T(8,128)}, f32[16,128,128]{2,1,0:T(8,128)S(1)}, u32[]{:S(2)}, u32[]{:S(2)}) collective-permute-start(f32[16,128,128]{2,1,0:T(8,128)} %add.628), channel_id=1, source_target_pairs={{0,1},{1,2},{2,3},{3,4},{4,5},{5,6},{6,7},{7,8},{8,9},{9,10},{10,1... | collective-permute-start | bytes 3145736 | tf_op jit(solution)/shard_map/while/body/eval_jaxpr/ppermute | solution.py:17
  533.6 16.0 %collective-permute-start = (f32[16,128,128]{2,1,0:T(8,128)}, f32[16,128,128]{2,1,0:T(8,128)S(1)}, u32[]{:S(2)}, u32[]{:S(2)}) collective-permute-start(f32[16,128,128]{2,1,0:T(8,128)} %add.628), channel_id=1, source_target_pairs={{0,1},{1,2},{2,3},{3,4},{4,5},{5,6},{6,7},{7,8},{8,9},{9,10},{10,1... | collective-permute-start | bytes 3145736 | tf_op jit(solution)/shard_map/while/body/eval_jaxpr/ppermute | solution.py:17
  553.1 16.0 %collective-permute-start = (f32[16,128,128]{2,1,0:T(8,128)}, f32[16,128,128]{2,1,0:T(8,128)S(1)}, u32[]{:S(2)}, u32[]{:S(2)}) collective-permute-start(f32[16,128,128]{2,1,0:T(8,128)} %add.628), channel_id=1, source_target_pairs={{0,1},{1,2},{2,3},{3,4},{4,5},{5,6},{6,7},{7,8},{8,9},{9,10},{10,1... | collective-permute-start | bytes 3145736 | tf_op jit(solution)/shard_map/while/body/eval_jaxpr/ppermute | solution.py:17
  572.6 16.0 %collective-permute-start = (f32[16,128,128]{2,1,0:T(8,128)}, f32[16,128,128]{2,1,0:T(8,128)S(1)}, u32[]{:S(2)}, u32[]{:S(2)}) collective-permute-start(f32[16,128,128]{2,1,0:T(8,128)} %add.628), channel_id=1, source_target_pairs={{0,1},{1,2},{2,3},{3,4},{4,5},{5,6},{6,7},{7,8},{8,9},{9,10},{10,1... | collective-permute-start | bytes 3145736 | tf_op jit(solution)/shard_map/while/body/eval_jaxpr/ppermute | solution.py:17
  597.9 72.7 %all-to-all-start.2 = ((bf16[32,256,128]{2,1,0:T(8,128)(2,1)}), bf16[32,256,128]{2,1,0:T(8,128)(2,1)S(1)}, u32[]{:S(2)}, u32[]{:S(2)}) async-start(bf16[32,256,128]{2,1,0:T(8,128)(2,1)} %bitcast.211), calls=%async_computation.2 | async-start | bytes 4194304 | tf_op jit(solution)/shard_map/all_to_all | solution.py:68
  784.4 17.0 %copy.103 = bf16[1,4096,128]{2,0,1:T(2,128)(2,1)} copy(bf16[1,4096,128]{2,1,0:T(8,128)(2,1)S(1)} %bitcast.216) | data formatting | bytes 2097152 | tf_op jit(solution)/shard_map/stack | solution.py:98
  801.9 24.7 %reduce.1 = bf16[4096,128]{1,0:T(8,128)(2,1)} reduce(bf16[4096,1,128]{2,1,0:T(2,128)(2,1)} %bitcast.212, bf16[]{:T(256)} %broadcast.649), dimensions={1}, to_apply=%bitcast.191.reduce_sub_computation | reduce | bytes 2097154
  (173 shorter events, 444.2 us)
Async XLA Ops:
  3.7 25.3 %all-to-all-start = ((bf16[32,128,128]{2,1,0:T(8,128)(2,1)}), bf16[32,128,128]{2,1,0:T(8,128)(2,1)}, u32[]{:S(2)}, u32[]{:S(2)}) async-start(bf16[32,128,128]{2,1,0:T(8,128)(2,1)} %bitcast.4), calls=%async_computation | async-start | bytes 2097152 | tf_op jit(solution)/shard_map/all_to_all | solution.py:66
  30.8 565.3 %all-to-all-start.1 = ((bf16[32,256,128]{2,1,0:T(8,128)(2,1)}), bf16[32,256,128]{2,1,0:T(8,128)(2,1)}, u32[]{:S(2)}, u32[]{:S(2)}) async-start(bf16[32,256,128]{2,1,0:T(8,128)(2,1)} %bitcast.8), calls=%async_computation.1 | async-start | bytes 4194304 | tf_op jit(solution)/shard_map/all_to_all | solution.py:67
  47.5 28.1 %collective-permute-start = (f32[16,128,128]{2,1,0:T(8,128)}, f32[16,128,128]{2,1,0:T(8,128)S(1)}, u32[]{:S(2)}, u32[]{:S(2)}) collective-permute-start(f32[16,128,128]{2,1,0:T(8,128)} %add.628), channel_id=1, source_target_pairs={{0,1},{1,2},{2,3},{3,4},{4,5},{5,6},{6,7},{7,8},{8,9},{9,10},{10,1... | collective-permute-start | bytes 3145736 | tf_op jit(solution)/shard_map/while/body/eval_jaxpr/ppermute | solution.py:17
  76.7 16.3 %collective-permute-start = (f32[16,128,128]{2,1,0:T(8,128)}, f32[16,128,128]{2,1,0:T(8,128)S(1)}, u32[]{:S(2)}, u32[]{:S(2)}) collective-permute-start(f32[16,128,128]{2,1,0:T(8,128)} %add.628), channel_id=1, source_target_pairs={{0,1},{1,2},{2,3},{3,4},{4,5},{5,6},{6,7},{7,8},{8,9},{9,10},{10,1... | collective-permute-start | bytes 3145736 | tf_op jit(solution)/shard_map/while/body/eval_jaxpr/ppermute | solution.py:17
  94.1 16.3 %collective-permute-start = (f32[16,128,128]{2,1,0:T(8,128)}, f32[16,128,128]{2,1,0:T(8,128)S(1)}, u32[]{:S(2)}, u32[]{:S(2)}) collective-permute-start(f32[16,128,128]{2,1,0:T(8,128)} %add.628), channel_id=1, source_target_pairs={{0,1},{1,2},{2,3},{3,4},{4,5},{5,6},{6,7},{7,8},{8,9},{9,10},{10,1... | collective-permute-start | bytes 3145736 | tf_op jit(solution)/shard_map/while/body/eval_jaxpr/ppermute | solution.py:17
  111.6 16.3 %collective-permute-start = (f32[16,128,128]{2,1,0:T(8,128)}, f32[16,128,128]{2,1,0:T(8,128)S(1)}, u32[]{:S(2)}, u32[]{:S(2)}) collective-permute-start(f32[16,128,128]{2,1,0:T(8,128)} %add.628), channel_id=1, source_target_pairs={{0,1},{1,2},{2,3},{3,4},{4,5},{5,6},{6,7},{7,8},{8,9},{9,10},{10,1... | collective-permute-start | bytes 3145736 | tf_op jit(solution)/shard_map/while/body/eval_jaxpr/ppermute | solution.py:17
  129.0 16.3 %collective-permute-start = (f32[16,128,128]{2,1,0:T(8,128)}, f32[16,128,128]{2,1,0:T(8,128)S(1)}, u32[]{:S(2)}, u32[]{:S(2)}) collective-permute-start(f32[16,128,128]{2,1,0:T(8,128)} %add.628), channel_id=1, source_target_pairs={{0,1},{1,2},{2,3},{3,4},{4,5},{5,6},{6,7},{7,8},{8,9},{9,10},{10,1... | collective-permute-start | bytes 3145736 | tf_op jit(solution)/shard_map/while/body/eval_jaxpr/ppermute | solution.py:17
  146.4 16.3 %collective-permute-start = (f32[16,128,128]{2,1,0:T(8,128)}, f32[16,128,128]{2,1,0:T(8,128)S(1)}, u32[]{:S(2)}, u32[]{:S(2)}) collective-permute-start(f32[16,128,128]{2,1,0:T(8,128)} %add.628), channel_id=1, source_target_pairs={{0,1},{1,2},{2,3},{3,4},{4,5},{5,6},{6,7},{7,8},{8,9},{9,10},{10,1... | collective-permute-start | bytes 3145736 | tf_op jit(solution)/shard_map/while/body/eval_jaxpr/ppermute | solution.py:17
  163.8 16.3 %collective-permute-start = (f32[16,128,128]{2,1,0:T(8,128)}, f32[16,128,128]{2,1,0:T(8,128)S(1)}, u32[]{:S(2)}, u32[]{:S(2)}) collective-permute-start(f32[16,128,128]{2,1,0:T(8,128)} %add.628), channel_id=1, source_target_pairs={{0,1},{1,2},{2,3},{3,4},{4,5},{5,6},{6,7},{7,8},{8,9},{9,10},{10,1... | collective-permute-start | bytes 3145736 | tf_op jit(solution)/shard_map/while/body/eval_jaxpr/ppermute | solution.py:17
  181.2 16.3 %collective-permute-start = (f32[16,128,128]{2,1,0:T(8,128)}, f32[16,128,128]{2,1,0:T(8,128)S(1)}, u32[]{:S(2)}, u32[]{:S(2)}) collective-permute-start(f32[16,128,128]{2,1,0:T(8,128)} %add.628), channel_id=1, source_target_pairs={{0,1},{1,2},{2,3},{3,4},{4,5},{5,6},{6,7},{7,8},{8,9},{9,10},{10,1... | collective-permute-start | bytes 3145736 | tf_op jit(solution)/shard_map/while/body/eval_jaxpr/ppermute | solution.py:17
  198.6 16.3 %collective-permute-start = (f32[16,128,128]{2,1,0:T(8,128)}, f32[16,128,128]{2,1,0:T(8,128)S(1)}, u32[]{:S(2)}, u32[]{:S(2)}) collective-permute-start(f32[16,128,128]{2,1,0:T(8,128)} %add.628), channel_id=1, source_target_pairs={{0,1},{1,2},{2,3},{3,4},{4,5},{5,6},{6,7},{7,8},{8,9},{9,10},{10,1... | collective-permute-start | bytes 3145736 | tf_op jit(solution)/shard_map/while/body/eval_jaxpr/ppermute | solution.py:17
  216.0 16.3 %collective-permute-start = (f32[16,128,128]{2,1,0:T(8,128)}, f32[16,128,128]{2,1,0:T(8,128)S(1)}, u32[]{:S(2)}, u32[]{:S(2)}) collective-permute-start(f32[16,128,128]{2,1,0:T(8,128)} %add.628), channel_id=1, source_target_pairs={{0,1},{1,2},{2,3},{3,4},{4,5},{5,6},{6,7},{7,8},{8,9},{9,10},{10,1... | collective-permute-start | bytes 3145736 | tf_op jit(solution)/shard_map/while/body/eval_jaxpr/ppermute | solution.py:17
  233.4 16.3 %collective-permute-start = (f32[16,128,128]{2,1,0:T(8,128)}, f32[16,128,128]{2,1,0:T(8,128)S(1)}, u32[]{:S(2)}, u32[]{:S(2)}) collective-permute-start(f32[16,128,128]{2,1,0:T(8,128)} %add.628), channel_id=1, source_target_pairs={{0,1},{1,2},{2,3},{3,4},{4,5},{5,6},{6,7},{7,8},{8,9},{9,10},{10,1... | collective-permute-start | bytes 3145736 | tf_op jit(solution)/shard_map/while/body/eval_jaxpr/ppermute | solution.py:17
  250.8 16.3 %collective-permute-start = (f32[16,128,128]{2,1,0:T(8,128)}, f32[16,128,128]{2,1,0:T(8,128)S(1)}, u32[]{:S(2)}, u32[]{:S(2)}) collective-permute-start(f32[16,128,128]{2,1,0:T(8,128)} %add.628), channel_id=1, source_target_pairs={{0,1},{1,2},{2,3},{3,4},{4,5},{5,6},{6,7},{7,8},{8,9},{9,10},{10,1... | collective-permute-start | bytes 3145736 | tf_op jit(solution)/shard_map/while/body/eval_jaxpr/ppermute | solution.py:17
  268.3 16.3 %collective-permute-start = (f32[16,128,128]{2,1,0:T(8,128)}, f32[16,128,128]{2,1,0:T(8,128)S(1)}, u32[]{:S(2)}, u32[]{:S(2)}) collective-permute-start(f32[16,128,128]{2,1,0:T(8,128)} %add.628), channel_id=1, source_target_pairs={{0,1},{1,2},{2,3},{3,4},{4,5},{5,6},{6,7},{7,8},{8,9},{9,10},{10,1... | collective-permute-start | bytes 3145736 | tf_op jit(solution)/shard_map/while/body/eval_jaxpr/ppermute | solution.py:17
  355.3 16.3 %collective-permute-start = (f32[16,128,128]{2,1,0:T(8,128)}, f32[16,128,128]{2,1,0:T(8,128)S(1)}, u32[]{:S(2)}, u32[]{:S(2)}) collective-permute-start(f32[16,128,128]{2,1,0:T(8,128)} %add.628), channel_id=1, source_target_pairs={{0,1},{1,2},{2,3},{3,4},{4,5},{5,6},{6,7},{7,8},{8,9},{9,10},{10,1... | collective-permute-start | bytes 3145736 | tf_op jit(solution)/shard_map/while/body/eval_jaxpr/ppermute | solution.py:17
  372.7 16.3 %collective-permute-start = (f32[16,128,128]{2,1,0:T(8,128)}, f32[16,128,128]{2,1,0:T(8,128)S(1)}, u32[]{:S(2)}, u32[]{:S(2)}) collective-permute-start(f32[16,128,128]{2,1,0:T(8,128)} %add.628), channel_id=1, source_target_pairs={{0,1},{1,2},{2,3},{3,4},{4,5},{5,6},{6,7},{7,8},{8,9},{9,10},{10,1... | collective-permute-start | bytes 3145736 | tf_op jit(solution)/shard_map/while/body/eval_jaxpr/ppermute | solution.py:17
  494.6 18.4 %collective-permute-start = (f32[16,128,128]{2,1,0:T(8,128)}, f32[16,128,128]{2,1,0:T(8,128)S(1)}, u32[]{:S(2)}, u32[]{:S(2)}) collective-permute-start(f32[16,128,128]{2,1,0:T(8,128)} %add.628), channel_id=1, source_target_pairs={{0,1},{1,2},{2,3},{3,4},{4,5},{5,6},{6,7},{7,8},{8,9},{9,10},{10,1... | collective-permute-start | bytes 3145736 | tf_op jit(solution)/shard_map/while/body/eval_jaxpr/ppermute | solution.py:17
  514.1 18.4 %collective-permute-start = (f32[16,128,128]{2,1,0:T(8,128)}, f32[16,128,128]{2,1,0:T(8,128)S(1)}, u32[]{:S(2)}, u32[]{:S(2)}) collective-permute-start(f32[16,128,128]{2,1,0:T(8,128)} %add.628), channel_id=1, source_target_pairs={{0,1},{1,2},{2,3},{3,4},{4,5},{5,6},{6,7},{7,8},{8,9},{9,10},{10,1... | collective-permute-start | bytes 3145736 | tf_op jit(solution)/shard_map/while/body/eval_jaxpr/ppermute | solution.py:17
  533.6 18.4 %collective-permute-start = (f32[16,128,128]{2,1,0:T(8,128)}, f32[16,128,128]{2,1,0:T(8,128)S(1)}, u32[]{:S(2)}, u32[]{:S(2)}) collective-permute-start(f32[16,128,128]{2,1,0:T(8,128)} %add.628), channel_id=1, source_target_pairs={{0,1},{1,2},{2,3},{3,4},{4,5},{5,6},{6,7},{7,8},{8,9},{9,10},{10,1... | collective-permute-start | bytes 3145736 | tf_op jit(solution)/shard_map/while/body/eval_jaxpr/ppermute | solution.py:17
  553.1 18.4 %collective-permute-start = (f32[16,128,128]{2,1,0:T(8,128)}, f32[16,128,128]{2,1,0:T(8,128)S(1)}, u32[]{:S(2)}, u32[]{:S(2)}) collective-permute-start(f32[16,128,128]{2,1,0:T(8,128)} %add.628), channel_id=1, source_target_pairs={{0,1},{1,2},{2,3},{3,4},{4,5},{5,6},{6,7},{7,8},{8,9},{9,10},{10,1... | collective-permute-start | bytes 3145736 | tf_op jit(solution)/shard_map/while/body/eval_jaxpr/ppermute | solution.py:17
  572.6 18.4 %collective-permute-start = (f32[16,128,128]{2,1,0:T(8,128)}, f32[16,128,128]{2,1,0:T(8,128)S(1)}, u32[]{:S(2)}, u32[]{:S(2)}) collective-permute-start(f32[16,128,128]{2,1,0:T(8,128)} %add.628), channel_id=1, source_target_pairs={{0,1},{1,2},{2,3},{3,4},{4,5},{5,6},{6,7},{7,8},{8,9},{9,10},{10,1... | collective-permute-start | bytes 3145736 | tf_op jit(solution)/shard_map/while/body/eval_jaxpr/ppermute | solution.py:17
  597.9 116.9 %all-to-all-start.2 = ((bf16[32,256,128]{2,1,0:T(8,128)(2,1)}), bf16[32,256,128]{2,1,0:T(8,128)(2,1)S(1)}, u32[]{:S(2)}, u32[]{:S(2)}) async-start(bf16[32,256,128]{2,1,0:T(8,128)(2,1)} %bitcast.211), calls=%async_computation.2 | async-start | bytes 4194304 | tf_op jit(solution)/shard_map/all_to_all | solution.py:68
  828.7 27.7 %all-to-all-start.3 = ((bf16[32,2,8192]{2,1,0:T(2,128)(2,1)}), bf16[32,2,8192]{2,1,0:T(2,128)(2,1)}, u32[]{:S(2)}, u32[]{:S(2)}) async-start(bf16[32,2,8192]{2,1,0:T(2,128)(2,1)} %reshape.577), calls=%async_computation.3 | async-start | bytes 2097152 | tf_op jit(solution)/shard_map/all_to_all | solution.py:99
  (30 other events, 942.8 us)
where the time goes:
time: 870 us; the launch traced here: 863 us
  starting transfers between devices  535 us (61%)
  matrix products  95.3 us (11%)
  waiting for transfers between devices  91.2 us (10%)
  other arithmetic  89.2 us (10%)
  local copies, waits for them, and re-layouts  40.3 us (5%)
  blocking collectives  10.5 us (1%)
    ppermute x31, starting transfers between devices, from_behind(): return lax.ppermute(value, axis, pairs)  441 us
    ppermute x31, waiting for transfers between devices, from_behind(): return lax.ppermute(value, axis, pairs)  74.7 us
    all_to_all x1, starting transfers between devices, shards(): lax.all_to_all(head_pieces(soft_v), 'seq', split_axis=0, concat_axis=1, t...  72.7 us
    dot_general x8, matrix products, shards(): jnp.einsum('qd,kd->qk', block_q, block_k, preferred_element_type=jnp.floa...  52.8 us
    add x31, other arithmetic, relay_step(): return from_behind(running + own_state, 'seq', 1)  33.9 us
    dot_general x8, matrix products, shards(): numerator = jnp.dot(weights, block_v, preferred_element_type=jnp.float32)  29.5 us
    reduce_sum x8, other arithmetic, shards(): denominator = jnp.sum(exponent, axis=1, keepdims=True)  29.3 us
    unnamed x4, other arithmetic  24.7 us
  transfers between devices with their start and end apart: 35, of which 32 were waited for; matrix products, arithmetic and copies ran while one was open for 11% of the time, Pallas kernels for 0%

commit v1 on v0

v1 whole, which is shorter than its diff:
```python
import functools

import jax
import jax.numpy as jnp
from jax import lax
from jax.experimental import pallas as pl
from jax.experimental.pallas import tpu as pltpu
from jax.sharding import PartitionSpec as P

HEADS = 64
HEAD_DIM = 128
EPSILON = 1e-06
MESH = pl.DeviceIdType.MESH
F32 = jnp.float32
BF16 = jnp.bfloat16

CHIPS = 16
SIDE = 4
ROWS = 256
SEQ = 8192
CHUNK = 1024
SCALE = HEAD_DIM ** -0.5
LOG2E = 1.4426950408889634


def kernel(
    lin_q, lin_k, lin_v, gain, soft_q, soft_k, soft_v,
    lin_out, soft_out,
    lq, lk, lv, mixed, state, half_in, chip_half, gathered, prefix_half, half_out, half_got,
    squares, kbuf, vbuf, qbuf, obuf, sbuf, pbuf, lbuf, mbuf,
    load_sem, k_send, k_recv, k_fwd, v_send, v_recv, v_fwd, q_send, q_recv, o_send, o_recv,
    x_sem, one_send, one_recv, two_send, two_recv, sq_send, sq_recv,
):
    me = lax.axis_index("seq")
    grp = lax.axis_index("grp")
    chip, core = me // 2, me % 2
    partner = chip * 2 + 1 - core
    y, z = chip // SIDE, chip % SIDE

    def chip_to(i):
        return (y + i // SIDE + i) % SIDE * SIDE + (z + i) % SIDE

    def chip_from(i):
        return (y + 2 * SIDE * SIDE - i // SIDE - i) % SIDE * SIDE + (z + SIDE * SIDE - i) % SIDE

    def cols(h):
        return pl.ds(pl.multiple_of(h * HEAD_DIM, HEAD_DIM), HEAD_DIM)

    def remote(src, dst, send, recv, seq):
        return pltpu.make_async_remote_copy(
            src_ref=src, dst_ref=dst, send_sem=send, recv_sem=recv,
            device_id={"seq": seq}, device_id_type=MESH)

    def arrived(dst, sem):
        pltpu.make_async_copy(dst, dst, sem).wait()

    loads = [pltpu.make_async_copy(src, dst, load_sem.at[n])
             for n, (src, dst) in enumerate(((lin_q, lq), (lin_k, lk), (lin_v, lv)))]
    for load in loads:
        load.start()

    barrier = pltpu.get_barrier_semaphore()

    @pl.loop(1, 2 * CHIPS)
    def _(i):
        pl.semaphore_signal(barrier, inc=1, device_id={"seq": lax.rem(me + i, 2 * CHIPS)}, device_id_type=MESH)

    for i in range(1, 4):
        pl.semaphore_signal(barrier, inc=1, device_id={"grp": lax.rem(grp + i, 4)}, device_id_type=MESH)

    for load in loads:
        load.wait()

    @pl.loop(0, CHIPS)
    def _(h):
        keys, values = lk[:, cols(h)], lv[:, cols(h)]
        state[h] = lax.dot_general(keys, values, (((0,), (0,)), ((), ())), preferred_element_type=F32)
        scores = lax.dot_general(lq[:, cols(h)], keys, (((1,), (1,)), ((), ())), preferred_element_type=F32)
        row = lax.broadcasted_iota(jnp.int32, (ROWS, ROWS), 0)
        col = lax.broadcasted_iota(jnp.int32, (ROWS, ROWS), 1)
        scores = jnp.where(col <= row, scores, 0.0)
        high = scores.astype(BF16)
        low = (scores - high.astype(F32)).astype(BF16)
        mixed[:, cols(h)] = (jnp.dot(high, values, preferred_element_type=F32)
                             + jnp.dot(low, values, preferred_element_type=F32))

    pl.semaphore_wait(barrier, 2 * CHIPS - 1 + 3)

    away = pl.ds(pl.multiple_of((1 - core) * 64, 64), 64)
    home = pl.ds(pl.multiple_of(core * 64, 64), 64)
    swap = remote(state.at[:, away, :], half_in, x_sem.at[0], x_sem.at[1], partner)
    swap.start()

    def spread(src, buf, send, recv, fwd):
        pltpu.make_async_copy(src.at[:, cols(chip)], buf.at[me], recv.at[me]).start()
        remote(src.at[:, cols(chip)], buf.at[me], fwd.at[0], recv.at[me], partner).start()

        @pl.loop(1, CHIPS)
        def _(i):
            c = chip_to(i)
            remote(src.at[:, cols(c)], buf.at[me], send.at[i], recv.at[me], 2 * c + core).start()

    def forward(buf, recv, fwd):
        @pl.loop(1, CHIPS)
        def _(i):
            s = 2 * chip_from(i) + core
            arrived(buf.at[s], recv.at[s])
            remote(buf.at[s], buf.at[s], fwd.at[i], recv.at[s], partner).start()

        arrived(buf.at[me], recv.at[me])

        @pl.loop(0, CHIPS)
        def _(i):
            s = 2 * chip_from(i) + 1 - core
            arrived(buf.at[s], recv.at[s])

    def sent(buf, src, send, fwd):
        remote(src.at[:, cols(chip)], buf.at[me], fwd.at[0], fwd.at[0], partner).wait_send()

        @pl.loop(1, CHIPS)
        def _(i):
            remote(src.at[:, cols(0)], buf.at[me], send.at[i], send.at[i], partner).wait_send()
            remote(buf.at[me], buf.at[me], fwd.at[i], fwd.at[i], partner).wait_send()

    spread(soft_k, kbuf, k_send, k_recv, k_fwd)

    q_core = (core + chip) % 2

    @pl.when(q_core == core)
    def _():
        pltpu.make_async_copy(soft_q.at[:, cols(chip)], qbuf.at[chip], q_recv.at[chip]).start()

    @pl.when(q_core != core)
    def _():
        remote(soft_q.at[:, cols(chip)], qbuf.at[chip], q_send.at[0], q_recv.at[chip], partner).start()

    @pl.loop(1, CHIPS)
    def _(i):
        c = chip_to(i)
        remote(soft_q.at[:, cols(c)], qbuf.at[chip], q_send.at[i], q_recv.at[chip], 2 * c + q_core).start()

    swap.wait()

    @pl.loop(0, CHIPS)
    def _(h):
        total = state[h, home, :] + half_in[h]
        chip_half[h] = total

        @pl.when(h == chip)
        def _():
            gathered[h] = total

    @pl.loop(1, CHIPS)
    def _(i):
        c = chip_to(i)
        remote(chip_half.at[c], gathered.at[chip], one_send.at[i], one_recv.at[chip], 2 * c + core).start()

    spread(soft_v, vbuf, v_send, v_recv, v_fwd)
    forward(kbuf, k_recv, k_fwd)

    def position(b):
        return 2 * b + (b + core) % 2

    def first_chunk(b):
        pair = b // 2
        return pair * (pair + 1) + b % 2 * (pair + 1)

    @pl.loop(0, CHIPS)
    def _(i):
        b = chip_from(i)
        s = position(b)
        chunks = b // 2 + 1
        base = first_chunk(b)
        arrived(qbuf.at[b], q_recv.at[b])
        queries = qbuf[b]
        mbuf[...] = jnp.full((ROWS, 128), -1e30, F32)

        def score(t, last):
            keys = kbuf[pl.ds(t * 4, 4)].reshape(CHUNK, HEAD_DIM)
            value = lax.dot_general(queries, keys, (((1,), (1,)), ((), ())), preferred_element_type=F32)
            if last:
                row = lax.broadcasted_iota(jnp.int32, (ROWS, CHUNK), 0) + s * ROWS
                col = lax.broadcasted_iota(jnp.int32, (ROWS, CHUNK), 1) + t * CHUNK
                value = jnp.where(col <= row, value, -1e30)
            sbuf[t] = value
            top = mbuf[...]
            for n in range(CHUNK // 128):
                top = jnp.maximum(top, value[:, n * 128:(n + 1) * 128])
            mbuf[...] = top

        @pl.loop(0, chunks - 1)
        def _(t):
            score(t, False)

        score(chunks - 1, True)
        top = jnp.max(mbuf[...], axis=1, keepdims=True) * (SCALE * LOG2E)
        mbuf[...] = jnp.broadcast_to(top, (ROWS, 128))
        lbuf[b] = jnp.zeros((ROWS, 128), F32)

        @pl.loop(0, chunks)
        def _(t):
            top = mbuf[...]
            total = lbuf[b]
            for n in range(CHUNK // 128):
                part = slice(n * 128, (n + 1) * 128)
                expo = jnp.exp2(sbuf[t, :, part] * (SCALE * LOG2E) - top)
                total = total + expo
                pbuf[base + t, :, part] = expo.astype(BF16)
            lbuf[b] = total

        @pl.when(i == 8)
        def _():
            def running(c, total):
                @pl.when(c != chip)
                def _():
                    arrived(gathered.at[c], one_recv.at[c])

                own = gathered[c]
                gathered[c] = total

                @pl.when(c == chip)
                def _():
                    prefix_half[c] = total

                return total + own

            lax.fori_loop(0, CHIPS, running, jnp.zeros((64, HEAD_DIM), F32))

            @pl.loop(1, CHIPS)
            def _(i):
                c = chip_to(i)
                remote(gathered.at[c], prefix_half.at[chip], two_send.at[i], two_recv.at[chip], 2 * c + core).start()

        @pl.when(i == 12)
        def _():
            forward(vbuf, v_recv, v_fwd)

    @pl.loop(0, CHIPS)
    def _(i):
        b = chip_from(i)
        s = position(b)
        chunks = b // 2 + 1
        base = first_chunk(b)

        def step(t, acc):
            values = vbuf[pl.ds(t * 4, 4)].reshape(CHUNK, HEAD_DIM)
            return acc + jnp.dot(pbuf[base + t], values, preferred_element_type=F32)

        acc = lax.fori_loop(0, chunks, step, jnp.zeros((ROWS, HEAD_DIM), F32))
        obuf[b] = (acc / jnp.sum(lbuf[b], axis=1, keepdims=True)).astype(BF16)

        @pl.when(s == me)
        def _():
            pltpu.make_async_copy(obuf.at[b], soft_out.at[:, cols(chip)], o_recv.at[chip]).start()

        @pl.when(s != me)
        def _():
            remote(obuf.at[b], soft_out.at[:, cols(chip)], o_send.at[b], o_recv.at[chip], s).start()

    @pl.loop(0, CHIPS)
    def _(h):
        @pl.when(h != chip)
        def _():
            arrived(prefix_half.at[h], two_recv.at[h])

    first = jnp.where(core == 0, 1.0, 0.0).astype(F32)
    half_out[...] = prefix_half[...] + first * state[:, 0:64, :]
    swap_two = remote(half_out, half_got, x_sem.at[2], x_sem.at[3], partner)
    swap_two.start()
    state[:, home, :] = prefix_half[...] + (1.0 - first) * half_in[...]
    swap_two.wait()
    state[:, away, :] = half_got[...]
    squares[0] = jnp.zeros((ROWS, 128), F32)

    @pl.loop(0, CHIPS)
    def _(h):
        full = state[h]
        high = full.astype(BF16)
        low = (full - high.astype(F32)).astype(BF16)
        queries = lq[:, cols(h)]
        out = (mixed[:, cols(h)] + jnp.dot(queries, high, preferred_element_type=F32)
               + jnp.dot(queries, low, preferred_element_type=F32))
        mixed[:, cols(h)] = out
        squares[0] += out * out

    swaps = []
    for i in range(1, 4):
        copy = pltpu.make_async_remote_copy(
            src_ref=squares.at[0], dst_ref=squares.at[i], send_sem=sq_send.at[i], recv_sem=sq_recv.at[i],
            device_id={"grp": lax.rem(grp + i, 4)}, device_id_type=MESH)
        copy.start()
        swaps.append(copy)
    for copy in swaps:
        copy.wait()
    total = squares[0] + squares[1] + squares[2] + squares[3]
    inverse = lax.rsqrt(jnp.sum(total, axis=1, keepdims=True) / (HEADS * HEAD_DIM) + EPSILON)
    mbuf[...] = jnp.broadcast_to(inverse, (ROWS, 128))

    @pl.loop(0, CHIPS)
    def _(h):
        lk[:, cols(h)] = (mixed[:, cols(h)] * mbuf[...] * gain[:, cols(h)]).astype(BF16)

    store = pltpu.make_async_copy(lk, lin_out, load_sem.at[3])
    store.start()

    sent(kbuf, soft_k, k_send, k_fwd)
    sent(vbuf, soft_v, v_send, v_fwd)

    @pl.when(q_core != core)
    def _():
        remote(soft_q.at[:, cols(0)], qbuf.at[0], q_send.at[0], q_send.at[0], partner).wait_send()

    @pl.loop(1, CHIPS)
    def _(i):
        remote(soft_q.at[:, cols(0)], qbuf.at[0], q_send.at[i], q_send.at[i], partner).wait_send()
        remote(chip_half.at[0], chip_half.at[0], one_send.at[i], one_send.at[i], partner).wait_send()
        remote(chip_half.at[0], chip_half.at[0], two_send.at[i], two_send.at[i], partner).wait_send()

    @pl.loop(0, CHIPS)
    def _(b):
        @pl.when(position(b) != me)
        def _():
            remote(obuf.at[0], obuf.at[0], o_send.at[b], o_send.at[b], partner).wait_send()

        arrived(soft_out.at[:, cols(b)], o_recv.at[b])

    store.wait()


def shards(lin_q, lin_k, lin_v, lin_gain, soft_q, soft_k, soft_v):
    half = pltpu.VMEM((CHIPS, 64, HEAD_DIM), F32)
    tokens = pltpu.VMEM((ROWS, CHIPS * HEAD_DIM), BF16)
    dma = pltpu.SemaphoreType.DMA
    hbm = pl.BlockSpec(memory_space=pl.ANY)
    shape = jax.ShapeDtypeStruct(lin_q.shape, BF16)
    return pl.pallas_call(
        kernel,
        out_shape=(shape, shape),
        in_specs=[hbm, hbm, hbm, pl.BlockSpec(memory_space=pltpu.VMEM), hbm, hbm, hbm],
        out_specs=(hbm, hbm),
        scratch_shapes=[
            tokens, tokens, tokens,
            pltpu.VMEM((ROWS, CHIPS * HEAD_DIM), F32),
            pltpu.VMEM((CHIPS, HEAD_DIM, HEAD_DIM), F32),
            half, half, half, half, half, half,
            pltpu.VMEM((4, ROWS, 128), F32),
            pltpu.VMEM((2 * CHIPS, ROWS, HEAD_DIM), BF16),
            pltpu.VMEM((2 * CHIPS, ROWS, HEAD_DIM), BF16),
            pltpu.VMEM((CHIPS, ROWS, HEAD_DIM), BF16),
            pltpu.VMEM((CHIPS, ROWS, HEAD_DIM), BF16),
            pltpu.VMEM((SEQ // CHUNK, ROWS, CHUNK), F32),
            pltpu.VMEM((72, ROWS, CHUNK), BF16),
            pltpu.VMEM((CHIPS, ROWS, 128), F32),
            pltpu.VMEM((ROWS, 128), F32),
            dma((4,)),
            dma((CHIPS,)), dma((2 * CHIPS,)), dma((CHIPS,)),
            dma((CHIPS,)), dma((2 * CHIPS,)), dma((CHIPS,)),
            dma((CHIPS,)), dma((CHIPS,)),
            dma((CHIPS,)), dma((CHIPS,)),
            dma((4,)),
            dma((CHIPS,)), dma((CHIPS,)),
            dma((CHIPS,)), dma((CHIPS,)),
            dma((4,)), dma((4,)),
        ],
        compiler_params=pltpu.CompilerParams(
            collective_id=0, has_side_effects=True, vmem_limit_bytes=67043328),
    )(lin_q, lin_k, lin_v, lin_gain.reshape(1, -1), soft_q, soft_k, soft_v)


def solution(mesh):
    split = P("seq", "grp")
    return jax.shard_map(
        shards,
        mesh=mesh,
        in_specs=(split, split, split, P("grp"), split, split, split),
        out_specs=(split, split),
        check_vma=False,
    )
```

time: 870 us -> 124 us (0.14)
  the two profiles are of different devices: /device:TPU:0 before, /device:TPU:24 now
where the time goes in v1:
time: 124 us; the launch traced here: 123 us
  Pallas kernels  119 us (96%)
  local copies, waits for them, and re-layouts  3.37 us (3%)
    pallas_call x1, Pallas kernels, shards(): pl.pallas_call(kernel, out_shape=(shape, shape), in_specs=[hbm, hbm, hbm,...  119 us
    unnamed x4, local copies, waits for them, and re-layouts  3.37 us

profile of v1, /device:TPU:24, one launch (start us, length us, event | category | flops | bytes accessed | tf_op | source)
XLA Modules:
  0.0 123.3 jit_solution(1292139985606606442)
XLA Ops:
  0.6 119.3 %shard_map.86 = (bf16[256,2048]{1,0:T(8,128)(2,1)}, bf16[256,2048]{1,0:T(8,128)(2,1)}) custom-call(bf16[256,2048]{1,0:T(8,128)(2,1)} %lin_q.1, bf16[256,2048]{1,0:T(8,128)(2,1)} %lin_k.1, bf16[256,2048]{1,0:T(8,128)(2,1)} %lin_v.1, f32[1,2048]{1,0:T(1,128)} %bitcast.1, bf16[256,2048]{1,0:T(8,128)(2,1)} %soft_q.1, bf16[256,2048]{1,0:T(8,128)(2,1)} %soft_k.1, ...), custom_call_target="tpu_custom_call" | custom-call | tf_op jit(solution)/shard_map/pallas_call | solution.py:336
  120.0 0.0 copy-start
  120.0 2.4 %copy.11 = bf16[256,2048]{1,0:T(8,128)(2,1)} copy(bf16[256,2048]{1,0:T(8,128)(2,1)} %get-tuple-element.4) | data formatting | bytes 2097152
  122.4 0.0 copy-done
  122.4 1.0 copy.12
Async XLA Ops:
  120.0 2.4 %copy-start = (bf16[256,2048]{1,0:T(8,128)(2,1)S(1)}, bf16[256,2048]{1,0:T(8,128)(2,1)}, u32[]{:S(2)}) copy-start(bf16[256,2048]{1,0:T(8,128)(2,1)} %get-tuple-element.5) | copy-start | bytes 3145732

commit v2 on v1

--- a/solution.py
+++ b/solution.py
@@ -27,7 +27,7 @@
     lin_q, lin_k, lin_v, gain, soft_q, soft_k, soft_v,
     lin_out, soft_out,
     lq, lk, lv, mixed, state, half_in, chip_half, gathered, prefix_half, half_out, half_got,
-    squares, kbuf, vbuf, qbuf, obuf, sbuf, pbuf, lbuf, mbuf,
+    squares, kbuf, vbuf, qbuf, sbuf, pbuf, lbuf, mbuf,
     load_sem, k_send, k_recv, k_fwd, v_send, v_recv, v_fwd, q_send, q_recv, o_send, o_recv,
     x_sem, one_send, one_recv, two_send, two_recv, sq_send, sq_recv,
 ):
@@ -67,6 +67,56 @@
 
     for i in range(1, 4):
         pl.semaphore_signal(barrier, inc=1, device_id={"grp": lax.rem(grp + i, 4)}, device_id_type=MESH)
+
+    pl.semaphore_wait(barrier, 2 * CHIPS - 1 + 3)
+
+    def spread(src, buf, send, recv, fwd):
+        pltpu.make_async_copy(src.at[:, cols(chip)], buf.at[me], recv.at[me]).start()
+        remote(src.at[:, cols(chip)], buf.at[me], fwd.at[0], recv.at[me], partner).start()
+
+        @pl.loop(1, CHIPS)
+        def _(i):
+            c = chip_to(i)
+            remote(src.at[:, cols(c)], buf.at[me], send.at[i], recv.at[me], 2 * c + core).start()
+
+    def forward(buf, recv, fwd):
+        @pl.loop(1, CHIPS)
+        def _(i):
+            s = 2 * chip_from(i) + core
+            arrived(buf.at[s], recv.at[s])
+            remote(buf.at[s], buf.at[s], fwd.at[i], recv.at[s], partner).start()
+
+        arrived(buf.at[me], recv.at[me])
+
+        @pl.loop(0, CHIPS)
+        def _(i):
+            s = 2 * chip_from(i) + 1 - core
+            arrived(buf.at[s], recv.at[s])
+
+    def sent(buf, src, send, fwd):
+        remote(src.at[:, cols(chip)], buf.at[me], fwd.at[0], fwd.at[0], partner).wait_send()
+
+        @pl.loop(1, CHIPS)
+        def _(i):
+            remote(src.at[:, cols(0)], buf.at[me], send.at[i], send.at[i], partner).wait_send()
+            remote(buf.at[me], buf.at[me], fwd.at[i], fwd.at[i], partner).wait_send()
+
+    spread(soft_k, kbuf, k_send, k_recv, k_fwd)
+
+    q_core = (core + chip) % 2
+
+    @pl.when(q_core == core)
+    def _():
+        pltpu.make_async_copy(soft_q.at[:, cols(chip)], qbuf.at[chip], q_recv.at[chip]).start()
+
+    @pl.when(q_core != core)
+    def _():
+        remote(soft_q.at[:, cols(chip)], qbuf.at[chip], q_send.at[0], q_recv.at[chip], partner).start()
+
+    @pl.loop(1, CHIPS)
+    def _(i):
+        c = chip_to(i)
+        remote(soft_q.at[:, cols(c)], qbuf.at[chip], q_send.at[i], q_recv.at[chip], 2 * c + q_core).start()
 
     for load in loads:
         load.wait()
@@ -84,61 +134,11 @@
         mixed[:, cols(h)] = (jnp.dot(high, values, preferred_element_type=F32)
                              + jnp.dot(low, values, preferred_element_type=F32))
 
-    pl.semaphore_wait(barrier, 2 * CHIPS - 1 + 3)
-
     away = pl.ds(pl.multiple_of((1 - core) * 64, 64), 64)
     home = pl.ds(pl.multiple_of(core * 64, 64), 64)
     swap = remote(state.at[:, away, :], half_in, x_sem.at[0], x_sem.at[1], partner)
     swap.start()
 
-    def spread(src, buf, send, recv, fwd):
-        pltpu.make_async_copy(src.at[:, cols(chip)], buf.at[me], recv.at[me]).start()
-        remote(src.at[:, cols(chip)], buf.at[me], fwd.at[0], recv.at[me], partner).start()
-
-        @pl.loop(1, CHIPS)
-        def _(i):
-            c = chip_to(i)
-            remote(src.at[:, cols(c)], buf.at[me], send.at[i], recv.at[me], 2 * c + core).start()
-
-    def forward(buf, recv, fwd):
-        @pl.loop(1, CHIPS)
-        def _(i):
-            s = 2 * chip_from(i) + core
-            arrived(buf.at[s], recv.at[s])
-            remote(buf.at[s], buf.at[s], fwd.at[i], recv.at[s], partner).start()
-
-        arrived(buf.at[me], recv.at[me])
-
-        @pl.loop(0, CHIPS)
-        def _(i):
-            s = 2 * chip_from(i) + 1 - core
-            arrived(buf.at[s], recv.at[s])
-
-    def sent(buf, src, send, fwd):
-        remote(src.at[:, cols(chip)], buf.at[me], fwd.at[0], fwd.at[0], partner).wait_send()
-
-        @pl.loop(1, CHIPS)
-        def _(i):
-            remote(src.at[:, cols(0)], buf.at[me], send.at[i], send.at[i], partner).wait_send()
-            remote(buf.at[me], buf.at[me], fwd.at[i], fwd.at[i], partner).wait_send()
-
-    spread(soft_k, kbuf, k_send, k_recv, k_fwd)
-
-    q_core = (core + chip) % 2
-
-    @pl.when(q_core == core)
-    def _():
-        pltpu.make_async_copy(soft_q.at[:, cols(chip)], qbuf.at[chip], q_recv.at[chip]).start()
-
-    @pl.when(q_core != core)
-    def _():
-        remote(soft_q.at[:, cols(chip)], qbuf.at[chip], q_send.at[0], q_recv.at[chip], partner).start()
-
-    @pl.loop(1, CHIPS)
-    def _(i):
-        c = chip_to(i)
-        remote(soft_q.at[:, cols(c)], qbuf.at[chip], q_send.at[i], q_recv.at[chip], 2 * c + q_core).start()
-
     swap.wait()
 
     @pl.loop(0, CHIPS)
@@ -161,54 +161,69 @@
     def position(b):
         return 2 * b + (b + core) % 2
 
-    def first_chunk(b):
-        pair = b // 2
-        return pair * (pair + 1) + b % 2 * (pair + 1)
-
-    @pl.loop(0, CHIPS)
-    def _(i):
-        b = chip_from(i)
-        s = position(b)
-        chunks = b // 2 + 1
-        base = first_chunk(b)
-        arrived(qbuf.at[b], q_recv.at[b])
-        queries = qbuf[b]
-        mbuf[...] = jnp.full((ROWS, 128), -1e30, F32)
-
-        def score(t, last):
-            keys = kbuf[pl.ds(t * 4, 4)].reshape(CHUNK, HEAD_DIM)
-            value = lax.dot_general(queries, keys, (((1,), (1,)), ((), ())), preferred_element_type=F32)
-            if last:
-                row = lax.broadcasted_iota(jnp.int32, (ROWS, CHUNK), 0) + s * ROWS
-                col = lax.broadcasted_iota(jnp.int32, (ROWS, CHUNK), 1) + t * CHUNK
-                value = jnp.where(col <= row, value, -1e30)
-            sbuf[t] = value
-            top = mbuf[...]
-            for n in range(CHUNK // 128):
-                top = jnp.maximum(top, value[:, n * 128:(n + 1) * 128])
-            mbuf[...] = top
-
-        @pl.loop(0, chunks - 1)
-        def _(t):
-            score(t, False)
-
-        score(chunks - 1, True)
-        top = jnp.max(mbuf[...], axis=1, keepdims=True) * (SCALE * LOG2E)
+    def score(b, half, t, last, n, top):
+        value = lax.dot_general(qbuf[b], kbuf[t * 4 + n], (((1,), (1,)), ((), ())), preferred_element_type=F32)
+        if last:
+            row = lax.broadcasted_iota(jnp.int32, (ROWS, ROWS), 0) + position(b) * ROWS
+            col = lax.broadcasted_iota(jnp.int32, (ROWS, ROWS), 1) + (t * 4 + n) * ROWS
+            value = jnp.where(col <= row, value, -1e30)
+        sbuf[t + 1 - half, :, n * 256:(n + 1) * 256] = value
+        most = jnp.maximum(value[:, :128], value[:, 128:])
+        return most if top is None else jnp.maximum(top, most)
+
+    def weigh(b, t, base, half, n):
+        rows = slice(n * 64, (n + 1) * 64)
+        top = mbuf[rows]
+        total = lbuf[b, rows]
+        for c in range(CHUNK // 128):
+            part = slice(c * 128, (c + 1) * 128)
+            expo = jnp.exp2(sbuf[t + 1 - half, rows, part] * (SCALE * LOG2E) - top)
+            total = total + expo
+            pbuf[base + t, half * ROWS + n * 64:half * ROWS + (n + 1) * 64, part] = expo.astype(BF16)
+        lbuf[b, rows] = total
+
+    def step(even, odd, t, base, last):
+        top = None
+        for n in range(4):
+            if even is not None:
+                weigh(even, t, base, 0, n)
+            top = score(odd, 0 if even is None else 1, t, last, n, top)
+        lbuf[odd] = jnp.maximum(lbuf[odd], top)
+
+    def settle(b):
+        top = jnp.max(lbuf[b], axis=1, keepdims=True) * (SCALE * LOG2E)
         mbuf[...] = jnp.broadcast_to(top, (ROWS, 128))
         lbuf[b] = jnp.zeros((ROWS, 128), F32)
 
-        @pl.loop(0, chunks)
+    @pl.loop(0, CHIPS // 2)
+    def _(i):
+        pair = (chip // 2 + CHIPS // 2 - i) % (CHIPS // 2)
+        even, odd = 2 * pair, 2 * pair + 1
+        base = pair * (pair + 1) // 2
+        for b in (even, odd):
+            arrived(qbuf.at[b], q_recv.at[b])
+            lbuf[b] = jnp.full((ROWS, 128), -1e30, F32)
+
+        @pl.loop(0, pair)
         def _(t):
-            top = mbuf[...]
-            total = lbuf[b]
-            for n in range(CHUNK // 128):
-                part = slice(n * 128, (n + 1) * 128)
-                expo = jnp.exp2(sbuf[t, :, part] * (SCALE * LOG2E) - top)
-                total = total + expo
-                pbuf[base + t, :, part] = expo.astype(BF16)
-            lbuf[b] = total
-
-        @pl.when(i == 8)
+            step(None, even, t, base, False)
+
+        step(None, even, pair, base, True)
+        settle(even)
+
+        @pl.loop(0, pair)
+        def _(t):
+            step(even, odd, t, base, False)
+
+        step(even, odd, pair, base, True)
+        settle(odd)
+
+        @pl.loop(0, pair + 1)
+        def _(t):
+            for n in range(4):
+                weigh(odd, t, base, 1, n)
+
+        @pl.when(i == 4)
         def _():
             def running(c, total):
                 @pl.when(c != chip)
@@ -231,31 +246,34 @@
                 c = chip_to(i)
                 remote(gathered.at[c], prefix_half.at[chip], two_send.at[i], two_recv.at[chip], 2 * c + core).start()
 
-        @pl.when(i == 12)
+        @pl.when(i == 6)
         def _():
             forward(vbuf, v_recv, v_fwd)
 
-    @pl.loop(0, CHIPS)
-    def _(i):
-        b = chip_from(i)
-        s = position(b)
-        chunks = b // 2 + 1
-        base = first_chunk(b)
-
-        def step(t, acc):
+    @pl.loop(0, CHIPS // 2)
+    def _(i):
+        pair = (chip // 2 + CHIPS // 2 - i) % (CHIPS // 2)
+        base = pair * (pair + 1) // 2
+        sbuf[0:2, :, 0:128] = jnp.zeros((2, ROWS, HEAD_DIM), F32)
+
+        @pl.loop(0, pair + 1)
+        def _(t):
             values = vbuf[pl.ds(t * 4, 4)].reshape(CHUNK, HEAD_DIM)
-            return acc + jnp.dot(pbuf[base + t], values, preferred_element_type=F32)
-
-        acc = lax.fori_loop(0, chunks, step, jnp.zeros((ROWS, HEAD_DIM), F32))
-        obuf[b] = (acc / jnp.sum(lbuf[b], axis=1, keepdims=True)).astype(BF16)
-
-        @pl.when(s == me)
-        def _():
-            pltpu.make_async_copy(obuf.at[b], soft_out.at[:, cols(chip)], o_recv.at[chip]).start()
-
-        @pl.when(s != me)
-        def _():
-            remote(obuf.at[b], soft_out.at[:, cols(chip)], o_send.at[b], o_recv.at[chip], s).start()
+            out = jnp.dot(pbuf[base + t], values, preferred_element_type=F32)
+            sbuf[0:2, :, 0:128] += out.reshape(2, ROWS, HEAD_DIM)
+
+        for half in range(2):
+            b = 2 * pair + half
+            s = position(b)
+            qbuf[b] = (sbuf[half, :, 0:128] / jnp.sum(lbuf[b], axis=1, keepdims=True)).astype(BF16)
+
+            @pl.when(s == me)
+            def _():
+                pltpu.make_async_copy(qbuf.at[b], soft_out.at[:, cols(chip)], o_recv.at[chip]).start()
+
+            @pl.when(s != me)
+            def _():
+                remote(qbuf.at[b], soft_out.at[:, cols(chip)], o_send.at[b], o_recv.at[chip], s).start()
 
     @pl.loop(0, CHIPS)
     def _(h):
@@ -320,7 +338,7 @@
     def _(b):
         @pl.when(position(b) != me)
         def _():
-            remote(obuf.at[0], obuf.at[0], o_send.at[b], o_send.at[b], partner).wait_send()
+            remote(qbuf.at[0], qbuf.at[0], o_send.at[b], o_send.at[b], partner).wait_send()
 
         arrived(soft_out.at[:, cols(b)], o_recv.at[b])
 
@@ -347,9 +365,8 @@
             pltpu.VMEM((2 * CHIPS, ROWS, HEAD_DIM), BF16),
             pltpu.VMEM((2 * CHIPS, ROWS, HEAD_DIM), BF16),
             pltpu.VMEM((CHIPS, ROWS, HEAD_DIM), BF16),
-            pltpu.VMEM((CHIPS, ROWS, HEAD_DIM), BF16),
-            pltpu.VMEM((SEQ // CHUNK, ROWS, CHUNK), F32),
-            pltpu.VMEM((72, ROWS, CHUNK), BF16),
+            pltpu.VMEM((SEQ // CHUNK + 1, ROWS, CHUNK), F32),
+            pltpu.VMEM((36, 2 * ROWS, CHUNK), BF16),
             pltpu.VMEM((CHIPS, ROWS, 128), F32),
             pltpu.VMEM((ROWS, 128), F32),
             dma((4,)),

time: 124 us -> 111 us (0.90)
  the two profiles are of different devices: /device:TPU:24 before, /device:TPU:0 now
where the time goes in v2:
time: 111 us; the launch traced here: 109 us
  Pallas kernels  105 us (95%)
  local copies, waits for them, and re-layouts  3.37 us (3%)
    pallas_call x1, Pallas kernels, shards(): pl.pallas_call(kernel, out_shape=(shape, shape), in_specs=[hbm, hbm, hbm,...  105 us
    unnamed x4, local copies, waits for them, and re-layouts  3.37 us

profile of v2, /device:TPU:0, one launch (start us, length us, event | category | flops | bytes accessed | tf_op | source)
XLA Modules:
  0.0 108.9 jit_solution(14808728322572559248)
XLA Ops:
  0.6 104.9 %shard_map.86 = (bf16[256,2048]{1,0:T(8,128)(2,1)}, bf16[256,2048]{1,0:T(8,128)(2,1)}) custom-call(bf16[256,2048]{1,0:T(8,128)(2,1)} %lin_q.1, bf16[256,2048]{1,0:T(8,128)(2,1)} %lin_k.1, bf16[256,2048]{1,0:T(8,128)(2,1)} %lin_v.1, f32[1,2048]{1,0:T(1,128)} %bitcast.1, bf16[256,2048]{1,0:T(8,128)(2,1)} %soft_q.1, bf16[256,2048]{1,0:T(8,128)(2,1)} %soft_k.1, ...), custom_call_target="tpu_custom_call" | custom-call | tf_op jit(solution)/shard_map/pallas_call | solution.py:354
  105.5 0.0 copy-start
  105.5 2.4 %copy.11 = bf16[256,2048]{1,0:T(8,128)(2,1)} copy(bf16[256,2048]{1,0:T(8,128)(2,1)} %get-tuple-element.4) | data formatting | bytes 2097152
  107.9 0.0 copy-done
  107.9 1.0 copy.12
Async XLA Ops:
  105.5 2.4 %copy-start = (bf16[256,2048]{1,0:T(8,128)(2,1)S(1)}, bf16[256,2048]{1,0:T(8,128)(2,1)}, u32[]{:S(2)}) copy-start(bf16[256,2048]{1,0:T(8,128)(2,1)} %get-tuple-element.5) | copy-start | bytes 3145732

commit v3 on v2

--- a/solution.py
+++ b/solution.py
@@ -43,6 +43,13 @@
     def chip_from(i):
         return (y + 2 * SIDE * SIDE - i // SIDE - i) % SIDE * SIDE + (z + SIDE * SIDE - i) % SIDE
 
+    def pair_from(i):
+        return (y + 12 - i // 2 * 3 - i % 2 * 2) % SIDE * 2 + (z // 2 + i) % 2
+
+    def query_to(j):
+        i = j // 2
+        return (y + i // 2 * 3 + i % 2 * 2) % SIDE * SIDE + (z // 2 + i) % 2 * 2 + j % 2
+
     def cols(h):
         return pl.ds(pl.multiple_of(h * HEAD_DIM, HEAD_DIM), HEAD_DIM)
 
@@ -113,10 +120,13 @@
     def _():
         remote(soft_q.at[:, cols(chip)], qbuf.at[chip], q_send.at[0], q_recv.at[chip], partner).start()
 
-    @pl.loop(1, CHIPS)
-    def _(i):
-        c = chip_to(i)
-        remote(soft_q.at[:, cols(c)], qbuf.at[chip], q_send.at[i], q_recv.at[chip], 2 * c + q_core).start()
+    beside = chip + 1 - chip % 2 * 2
+    remote(soft_q.at[:, cols(beside)], qbuf.at[chip], q_send.at[1], q_recv.at[chip], 2 * beside + q_core).start()
+
+    @pl.loop(2, CHIPS)
+    def _(j):
+        c = query_to(j)
+        remote(soft_q.at[:, cols(c)], qbuf.at[chip], q_send.at[j], q_recv.at[chip], 2 * c + q_core).start()
 
     for load in loads:
         load.wait()
@@ -172,21 +182,22 @@
         return most if top is None else jnp.maximum(top, most)
 
     def weigh(b, t, base, half, n):
-        rows = slice(n * 64, (n + 1) * 64)
+        rows = slice(n * 32, (n + 1) * 32)
         top = mbuf[rows]
         total = lbuf[b, rows]
         for c in range(CHUNK // 128):
             part = slice(c * 128, (c + 1) * 128)
             expo = jnp.exp2(sbuf[t + 1 - half, rows, part] * (SCALE * LOG2E) - top)
             total = total + expo
-            pbuf[base + t, half * ROWS + n * 64:half * ROWS + (n + 1) * 64, part] = expo.astype(BF16)
+            pbuf[base + t, half * ROWS + n * 32:half * ROWS + (n + 1) * 32, part] = expo.astype(BF16)
         lbuf[b, rows] = total
 
     def step(even, odd, t, base, last):
         top = None
+        if even is not None:
+            for n in range(8):
+                weigh(even, t, base, 0, n)
         for n in range(4):
-            if even is not None:
-                weigh(even, t, base, 0, n)
             top = score(odd, 0 if even is None else 1, t, last, n, top)
         lbuf[odd] = jnp.maximum(lbuf[odd], top)
 
@@ -197,7 +208,7 @@
 
     @pl.loop(0, CHIPS // 2)
     def _(i):
-        pair = (chip // 2 + CHIPS // 2 - i) % (CHIPS // 2)
+        pair = pair_from(i)
         even, odd = 2 * pair, 2 * pair + 1
         base = pair * (pair + 1) // 2
         for b in (even, odd):
@@ -220,7 +231,7 @@
 
         @pl.loop(0, pair + 1)
         def _(t):
-            for n in range(4):
+            for n in range(8):
                 weigh(odd, t, base, 1, n)
 
         @pl.when(i == 4)
@@ -250,9 +261,60 @@
         def _():
             forward(vbuf, v_recv, v_fwd)
 
+    @pl.loop(0, CHIPS)
+    def _(h):
+        @pl.when(h != chip)
+        def _():
+            arrived(prefix_half.at[h], two_recv.at[h])
+
+    first = jnp.where(core == 0, 1.0, 0.0).astype(F32)
+    half_out[...] = prefix_half[...] + first * state[:, 0:64, :]
+    state[:, home, :] = prefix_half[...] + (1.0 - first) * half_in[...]
+    swap_two = remote(half_out, half_got, x_sem.at[2], x_sem.at[3], partner)
+    swap_two.start()
+
+    def squares_to(i):
+        return pltpu.make_async_remote_copy(
+            src_ref=squares.at[0], dst_ref=squares.at[i], send_sem=sq_send.at[i], recv_sem=sq_recv.at[i],
+            device_id={"grp": lax.rem(grp + i, 4)}, device_id_type=MESH)
+
+    store = pltpu.make_async_copy(lk, lin_out, load_sem.at[3])
+
+    def carry():
+        swap_two.wait()
+        state[:, away, :] = half_got[...]
+        squares[0] = jnp.zeros((ROWS, 128), F32)
+
+        @pl.loop(0, CHIPS)
+        def _(h):
+            full = state[h]
+            high = full.astype(BF16)
+            low = (full - high.astype(F32)).astype(BF16)
+            queries = lq[:, cols(h)]
+            out = (mixed[:, cols(h)] + jnp.dot(queries, high, preferred_element_type=F32)
+                   + jnp.dot(queries, low, preferred_element_type=F32))
+            mixed[:, cols(h)] = out
+            squares[0] += out * out
+
+        for i in range(1, 4):
+            squares_to(i).start()
+
+    def normalize():
+        for i in range(1, 4):
+            squares_to(i).wait()
+        total = squares[0] + squares[1] + squares[2] + squares[3]
+        inverse = lax.rsqrt(jnp.sum(total, axis=1, keepdims=True) / (HEADS * HEAD_DIM) + EPSILON)
+        mbuf[...] = jnp.broadcast_to(inverse, (ROWS, 128))
+
+        @pl.loop(0, CHIPS)
+        def _(h):
+            lk[:, cols(h)] = (mixed[:, cols(h)] * mbuf[...] * gain[:, cols(h)]).astype(BF16)
+
+        store.start()
+
     @pl.loop(0, CHIPS // 2)
     def _(i):
-        pair = (chip // 2 + CHIPS // 2 - i) % (CHIPS // 2)
+        pair = pair_from(i)
         base = pair * (pair + 1) // 2
         sbuf[0:2, :, 0:128] = jnp.zeros((2, ROWS, HEAD_DIM), F32)
 
@@ -275,51 +337,8 @@
             def _():
                 remote(qbuf.at[b], soft_out.at[:, cols(chip)], o_send.at[b], o_recv.at[chip], s).start()
 
-    @pl.loop(0, CHIPS)
-    def _(h):
-        @pl.when(h != chip)
-        def _():
-            arrived(prefix_half.at[h], two_recv.at[h])
-
-    first = jnp.where(core == 0, 1.0, 0.0).astype(F32)
-    half_out[...] = prefix_half[...] + first * state[:, 0:64, :]
-    swap_two = remote(half_out, half_got, x_sem.at[2], x_sem.at[3], partner)
-    swap_two.start()
-    state[:, home, :] = prefix_half[...] + (1.0 - first) * half_in[...]
-    swap_two.wait()
-    state[:, away, :] = half_got[...]
-    squares[0] = jnp.zeros((ROWS, 128), F32)
-
-    @pl.loop(0, CHIPS)
-    def _(h):
-        full = state[h]
-        high = full.astype(BF16)
-        low = (full - high.astype(F32)).astype(BF16)
-        queries = lq[:, cols(h)]
-        out = (mixed[:, cols(h)] + jnp.dot(queries, high, preferred_element_type=F32)
-               + jnp.dot(queries, low, preferred_element_type=F32))
-        mixed[:, cols(h)] = out
-        squares[0] += out * out
-
-    swaps = []
-    for i in range(1, 4):
-        copy = pltpu.make_async_remote_copy(
-            src_ref=squares.at[0], dst_ref=squares.at[i], send_sem=sq_send.at[i], recv_sem=sq_recv.at[i],
-            device_id={"grp": lax.rem(grp + i, 4)}, device_id_type=MESH)
-        copy.start()
-        swaps.append(copy)
-    for copy in swaps:
-        copy.wait()
-    total = squares[0] + squares[1] + squares[2] + squares[3]
-    inverse = lax.rsqrt(jnp.sum(total, axis=1, keepdims=True) / (HEADS * HEAD_DIM) + EPSILON)
-    mbuf[...] = jnp.broadcast_to(inverse, (ROWS, 128))
-
-    @pl.loop(0, CHIPS)
-    def _(h):
-        lk[:, cols(h)] = (mixed[:, cols(h)] * mbuf[...] * gain[:, cols(h)]).astype(BF16)
-
-    store = pltpu.make_async_copy(lk, lin_out, load_sem.at[3])
-    store.start()
+        pl.when(i == 1)(carry)
+        pl.when(i == 4)(normalize)
 
     sent(kbuf, soft_k, k_send, k_fwd)
     sent(vbuf, soft_v, v_send, v_fwd)

time: 111 us -> 98.9 us (0.89); the launches traced: 109 us -> 98.7 us
  Pallas kernels: 105 us -> 94.7 us
    pallas_call x1, Pallas kernels: 105 us -> 94.7 us  [shards(): pl.pallas_call(kernel, out_shape=(shape, shape), in_specs=[hbm, hbm, hbm,...]
where the time goes in v3:
time: 98.9 us; the launch traced here: 98.7 us
  Pallas kernels  94.7 us (96%)
  local copies, waits for them, and re-layouts  3.37 us (3%)
    pallas_call x1, Pallas kernels, shards(): pl.pallas_call(kernel, out_shape=(shape, shape), in_specs=[hbm, hbm, hbm,...  94.7 us
    unnamed x4, local copies, waits for them, and re-layouts  3.37 us

profile of v3, /device:TPU:0, one launch (start us, length us, event | category | flops | bytes accessed | tf_op | source)
XLA Modules:
  0.0 98.7 jit_solution(3286821638205490859)
XLA Ops:
  0.6 94.7 %shard_map.86 = (bf16[256,2048]{1,0:T(8,128)(2,1)}, bf16[256,2048]{1,0:T(8,128)(2,1)}) custom-call(bf16[256,2048]{1,0:T(8,128)(2,1)} %lin_q.1, bf16[256,2048]{1,0:T(8,128)(2,1)} %lin_k.1, bf16[256,2048]{1,0:T(8,128)(2,1)} %lin_v.1, f32[1,2048]{1,0:T(1,128)} %bitcast.1, bf16[256,2048]{1,0:T(8,128)(2,1)} %soft_q.1, bf16[256,2048]{1,0:T(8,128)(2,1)} %soft_k.1, ...), custom_call_target="tpu_custom_call" | custom-call | tf_op jit(solution)/shard_map/pallas_call | solution.py:373
  95.4 0.0 copy-start
  95.4 2.4 %copy.11 = bf16[256,2048]{1,0:T(8,128)(2,1)} copy(bf16[256,2048]{1,0:T(8,128)(2,1)} %get-tuple-element.4) | data formatting | bytes 2097152
  97.8 0.0 copy-done
  97.8 1.0 copy.12
Async XLA Ops:
  95.4 2.4 %copy-start = (bf16[256,2048]{1,0:T(8,128)(2,1)S(1)}, bf16[256,2048]{1,0:T(8,128)(2,1)}, u32[]{:S(2)}) copy-start(bf16[256,2048]{1,0:T(8,128)(2,1)} %get-tuple-element.5) | copy-start | bytes 3145732

commit v4 on v3

--- a/solution.py
+++ b/solution.py
@@ -192,14 +192,15 @@
             pbuf[base + t, half * ROWS + n * 32:half * ROWS + (n + 1) * 32, part] = expo.astype(BF16)
         lbuf[b, rows] = total
 
-    def step(even, odd, t, base, last):
+    def weigh_all(b, t, base, half):
+        for n in range(8):
+            weigh(b, t, base, half, n)
+
+    def step(b, half, t, last):
         top = None
-        if even is not None:
-            for n in range(8):
-                weigh(even, t, base, 0, n)
         for n in range(4):
-            top = score(odd, 0 if even is None else 1, t, last, n, top)
-        lbuf[odd] = jnp.maximum(lbuf[odd], top)
+            top = score(b, half, t, last, n, top)
+        lbuf[b] = jnp.maximum(lbuf[b], top)
 
     def settle(b):
         top = jnp.max(lbuf[b], axis=1, keepdims=True) * (SCALE * LOG2E)
@@ -211,28 +212,39 @@
         pair = pair_from(i)
         even, odd = 2 * pair, 2 * pair + 1
         base = pair * (pair + 1) // 2
+        before = pair_from(jnp.maximum(i - 1, 0))
+        old, old_base = 2 * before + 1, before * (before + 1) // 2
+        left = jnp.where(i == 0, 0, before + 1)
+        both = jnp.minimum(pair, left)
         for b in (even, odd):
             arrived(qbuf.at[b], q_recv.at[b])
             lbuf[b] = jnp.full((ROWS, 128), -1e30, F32)
 
+        @pl.loop(0, left - both)
+        def _(t):
+            weigh_all(old, both + t, old_base, 1)
+
+        step(even, 0, pair, True)
+
+        @pl.loop(0, pair - both)
+        def _(t):
+            step(even, 0, both + t, False)
+
+        @pl.loop(0, both)
+        def _(t):
+            weigh_all(old, both - 1 - t, old_base, 1)
+            step(even, 0, both - 1 - t, False)
+
+        settle(even)
+
         @pl.loop(0, pair)
         def _(t):
-            step(None, even, t, base, False)
-
-        step(None, even, pair, base, True)
-        settle(even)
-
-        @pl.loop(0, pair)
-        def _(t):
-            step(even, odd, t, base, False)
-
-        step(even, odd, pair, base, True)
+            weigh_all(even, t, base, 0)
+            step(odd, 1, t, False)
+
+        weigh_all(even, pair, base, 0)
+        step(odd, 1, pair, True)
         settle(odd)
-
-        @pl.loop(0, pair + 1)
-        def _(t):
-            for n in range(8):
-                weigh(odd, t, base, 1, n)
 
         @pl.when(i == 4)
         def _():
@@ -260,6 +272,12 @@
         @pl.when(i == 6)
         def _():
             forward(vbuf, v_recv, v_fwd)
+
+    final = pair_from(CHIPS // 2 - 1)
+
+    @pl.loop(0, final + 1)
+    def _(t):
+        weigh_all(2 * final + 1, t, final * (final + 1) // 2, 1)
 
     @pl.loop(0, CHIPS)
     def _(h):
@@ -321,8 +339,8 @@
         @pl.loop(0, pair + 1)
         def _(t):
             values = vbuf[pl.ds(t * 4, 4)].reshape(CHUNK, HEAD_DIM)
-            out = jnp.dot(pbuf[base + t], values, preferred_element_type=F32)
-            sbuf[0:2, :, 0:128] += out.reshape(2, ROWS, HEAD_DIM)
+            for n in range(2):
+                sbuf[n, :, 0:128] += jnp.dot(pbuf[base + t, n * 256:(n + 1) * 256], values, preferred_element_type=F32)
 
         for half in range(2):
             b = 2 * pair + half

time: 98.9 us -> 97.8 us (0.989)
  Pallas kernels: 94.7 us -> 93.6 us
    pallas_call x1, Pallas kernels: 94.7 us -> 93.6 us  [shards(): pl.pallas_call(kernel, out_shape=(shape, shape), in_specs=[hbm, hbm, hbm,...]
where the time goes in v4:
time: 97.8 us; the launch traced here: 97.6 us
  Pallas kernels  93.6 us (96%)
  local copies, waits for them, and re-layouts  3.37 us (3%)
    pallas_call x1, Pallas kernels, shards(): pl.pallas_call(kernel, out_shape=(shape, shape), in_specs=[hbm, hbm, hbm,...  93.6 us
    unnamed x4, local copies, waits for them, and re-layouts  3.37 us

profile of v4, /device:TPU:0, one launch (start us, length us, event | category | flops | bytes accessed | tf_op | source)
XLA Modules:
  0.0 97.6 jit_solution(18217765788780133084)
XLA Ops:
  0.6 93.6 %shard_map.86 = (bf16[256,2048]{1,0:T(8,128)(2,1)}, bf16[256,2048]{1,0:T(8,128)(2,1)}) custom-call(bf16[256,2048]{1,0:T(8,128)(2,1)} %lin_q.1, bf16[256,2048]{1,0:T(8,128)(2,1)} %lin_k.1, bf16[256,2048]{1,0:T(8,128)(2,1)} %lin_v.1, f32[1,2048]{1,0:T(1,128)} %bitcast.1, bf16[256,2048]{1,0:T(8,128)(2,1)} %soft_q.1, bf16[256,2048]{1,0:T(8,128)(2,1)} %soft_k.1, ...), custom_call_target="tpu_custom_call" | custom-call | tf_op jit(solution)/shard_map/pallas_call | solution.py:391
  94.3 0.0 copy-start
  94.3 2.4 %copy.11 = bf16[256,2048]{1,0:T(8,128)(2,1)} copy(bf16[256,2048]{1,0:T(8,128)(2,1)} %get-tuple-element.4) | data formatting | bytes 2097152
  96.7 0.0 copy-done
  96.7 1.0 copy.12
Async XLA Ops:
  94.3 2.4 %copy-start = (bf16[256,2048]{1,0:T(8,128)(2,1)S(1)}, bf16[256,2048]{1,0:T(8,128)(2,1)}, u32[]{:S(2)}) copy-start(bf16[256,2048]{1,0:T(8,128)(2,1)} %get-tuple-element.5) | copy-start | bytes 3145732
